TPU v7x, 256 devices: a whole 4x4x8 slice. The times are simulated.
256 devices in a mesh: train: 16 (over z, core), query: 16 (over y, x).
Axes of the slice: x: 4, y: 4, z: 8, core: 2. Of those that a mesh axis runs over, the one named last changes fastest.
Arguments:
- train_hidden: bfloat16 [512, 96, 4096], P(('train', 'query')), may hold values from -6 to 6
- train_outgrad: bfloat16 [512, 96, 14336], P(('train', 'query')), may hold values from -6 to 6
- train_mask: int32 [512, 96], P(('train', 'query')), may hold values 0 or 1
- query_hidden: bfloat16 [256, 96, 4096], P(('train', 'query')), may hold values from -6 to 6
- query_outgrad: bfloat16 [256, 96, 14336], P(('train', 'query')), may hold values from -6 to 6
- query_mask: int32 [256, 96], P(('train', 'query')), may hold values 0 or 1
- proj_in: bfloat16 [4096, 64], replicated, may hold values from -0.09375 to 0.09375
- proj_out: bfloat16 [14336, 64], replicated, may hold values from -0.046875 to 0.046875
Outputs:
- scores: float32 [512, 256], P(('train', 'query'))
All inputs are finite; a program needn't handle non-finite values. No bound on the sum of `train_mask` or of `query_mask` on one device may be relied on, other than what follows from the above.
Results may differ from a plain program's by a relative error of at most 0.0003.
Values sent between devices are 32-bit elements; how exact they have to be, the bound alone decides.
A program may use at most 128 MiB of HBM per device.

v0:
```python
import jax
import jax.numpy as jnp
from jax import lax
from jax.sharding import PartitionSpec as P

damping_share = 0.1
AXES = ("train", "query")
HIGHEST = lax.Precision.HIGHEST


def sketch_terms(hidden, outgrad, mask, proj_in, proj_out):
    proof_count, token_count, model_width = hidden.shape
    input_side = jnp.dot(
        hidden.reshape(proof_count * token_count, model_width),
        proj_in,
        preferred_element_type=jnp.float32,
    )
    output_side = jnp.dot(
        outgrad.reshape(proof_count * token_count, -1), proj_out, preferred_element_type=jnp.float32
    )
    output_side = output_side * mask.reshape(-1, 1).astype(jnp.float32)
    input_side = input_side.reshape(proof_count, token_count, -1)
    output_side = output_side.reshape(proof_count, token_count, -1)
    outer_sum = jnp.einsum("pti,ptj->pij", output_side, input_side, precision=HIGHEST)
    return outer_sum.reshape(proof_count, -1)


def spd_solve(system, right, tolerance=0.001, most_steps=48):
    size = system.shape[0]
    eye = jnp.eye(size, dtype=system.dtype)
    diagonal = jnp.sum(system * eye, axis=1)
    inv_sqrt = lax.rsqrt(diagonal)
    bound = jnp.max(jnp.sum(jnp.abs(system) * inv_sqrt[:, None] * inv_sqrt[None, :], axis=1))
    start = eye * (1.0 / (diagonal * bound))[None, :]

    def going(carry):
        step, _, residual = carry
        return (step < most_steps) & (residual > tolerance)

    def one_step(inverse):
        remainder = eye - jnp.dot(system, inverse, precision=HIGHEST)
        residual = jnp.sqrt(jnp.sum(remainder * remainder))
        return (inverse + jnp.dot(inverse, remainder, precision=HIGHEST), residual)

    def advance(carry):
        step, inverse, _ = carry
        for _ in range(3):
            inverse, _ = one_step(inverse)
        inverse, residual = one_step(inverse)
        return (step + 4, inverse, residual)

    _, inverse, _ = lax.while_loop(
        going, advance, (jnp.int32(0), start, jnp.array(jnp.inf, system.dtype))
    )
    solved = jnp.dot(inverse, right, precision=HIGHEST)
    return solved + jnp.dot(
        inverse, right - jnp.dot(system, solved, precision=HIGHEST), precision=HIGHEST
    )


def body(
    train_hidden,
    train_outgrad,
    train_mask,
    query_hidden,
    query_outgrad,
    query_mask,
    proj_in,
    proj_out,
):
    train_sketch = sketch_terms(train_hidden, train_outgrad, train_mask, proj_in, proj_out)
    query_sketch = sketch_terms(query_hidden, query_outgrad, query_mask, proj_in, proj_out)
    block_rows = train_sketch.shape[0]
    width = train_sketch.shape[1]
    both = jnp.concatenate([train_sketch, query_sketch], axis=0)
    within = lax.all_gather(both.reshape(1, -1), AXES[1], axis=0, tiled=True)
    everyone = lax.all_gather(within, AXES[0], axis=0, tiled=True)
    devices = everyone.shape[0]
    pieces = [everyone[:, r * width : (r + 1) * width] for r in range(block_rows + 1)]
    all_train = jnp.concatenate(pieces[:block_rows], axis=0)
    gram_matrix = jnp.dot(all_train, all_train.T, precision=HIGHEST)
    products = jnp.dot(all_train, pieces[block_rows].T, precision=HIGHEST)
    total_rows = gram_matrix.shape[0]
    eye = jnp.eye(total_rows, dtype=jnp.float32)
    damping = damping_share * jnp.sum(gram_matrix * eye) / total_rows
    system = gram_matrix + damping * eye
    system, products = lax.optimization_barrier((system, products))
    solved = total_rows * spd_solve(system, products)
    me = lax.axis_index(AXES)
    return jnp.concatenate(
        [lax.dynamic_slice_in_dim(solved, r * devices + me, 1, 0) for r in range(block_rows)],
        axis=0,
    )


def solution(mesh):
    in_specs = (
        P(AXES, None, None),
        P(AXES, None, None),
        P(AXES, None),
        P(AXES, None, None),
        P(AXES, None, None),
        P(AXES, None),
        P(),
        P(),
    )
    out_specs = P(AXES, None)
    return jax.shard_map(body, mesh=mesh, in_specs=in_specs, out_specs=out_specs, check_vma=False)
```

profile of v0, /device:TPU:1, one launch (start us, length us, event | category | flops | bytes accessed | tf_op | source)
XLA Modules:
  0.0 246.9 jit_solution(12028360750653401418)
XLA Ops:
  9.8 2.4 fusion.9
  12.5 5.1 %convolution_multiply_fusion = f32[192,64]{0,1:T(8,128)S(1)} fusion(bf16[192,14336]{1,0:T(8,128)(2,1)} %bitcast.103, bf16[14336,64]{0,1:T(8,128)(2,1)} %param.17, f32[192]{0:T(256)S(1)} %convert_element_type.33), kind=kOutput, calls=%fused_computation.24 | convolution fusion | flops 352333824 | bytes 7389952 | tf_op jit(solution)/shard_map/dot_general | solution.py:18
  17.7 2.1 fusion.15
  20.2 20.5 %all-gather = f32[16,1,12288]{2,1,0:T(1,128)S(1)} all-gather(f32[1,1,12288]{2,1,0:T(1,128)S(1)} %reshape.68), channel_id=1, replica_groups=mesh['train'=16,'query'=16] {'query'}, dimensions={0}, use_global_device_ids=true | all-gather | bytes 835584 | tf_op jit(solution)/shard_map/all_gather | solution.py:76
  42.1 82.2 %all-gather.3.cloned.1.call-done = f32[256,12288]{1,0:T(8,128)} async-done(((f32[16,12288]{1,0:T(8,128)}), f32[256,12288]{1,0:T(8,128)}) %all-gather.3.cloned.1.call-update) | async-done | bytes 12582928 | tf_op jit(solution)/shard_map/all_gather | solution.py:77
  124.3 4.0 %fusion.21 = (f32[256,4096]{1,0:T(8,128)S(1)}, f32[256,4096]{1,0:T(8,128)S(1)}) fusion(f32[256,12288]{1,0:T(8,128)} %all-gather.3.cloned.1.call-done), kind=kLoop, calls=%fused_computation.47 | loop fusion | bytes 16777216 | tf_op jit(solution)/shard_map/slice | solution.py:79
  128.4 15.9 %select_reduce_fusion.1 = (f32[]{:T(128)}, f32[512,512]{1,0:T(8,128)}) fusion(f32[256,4096]{1,0:T(8,128)S(1)} %get-tuple-element.91, f32[256,4096]{1,0:T(8,128)S(1)} %get-tuple-element.90), kind=kOutput, calls=%fused_computation.29 | convolution fusion | flops 12887785472 | bytes 9437188 | tf_op jit(solution)/shard_map/dot_general | solution.py:81
  146.3 10.6 %fusion.3 = f32[512,256]{1,0:T(8,128)S(1)} fusion(f32[256,4096]{1,0:T(8,128)} %copy-done.6, f32[256,4096]{1,0:T(8,128)} %copy-done.5, f32[256,12288]{1,0:T(8,128)} %all-gather.3.cloned.1.call-done), kind=kOutput, calls=%fused_computation.16 | convolution fusion | flops 6444548096 | bytes 13107200 | tf_op jit(solution)/shard_map/dot_general | solution.py:82
  159.7 2.5 %copy.18 = f32[512,512]{0,1:T(8,128)} copy(f32[512,512]{1,0:T(8,128)} %fusion.12) | data formatting | bytes 2097152
  162.3 70.0 %while.14 = (s32[]{:T(128)}, f32[512,512]{0,1:T(8,128)}, f32[]{:T(128)}, f32[512,512]{1,0:T(8,128)}, s32[]{:T(128)}) while((s32[]{:T(128)}, f32[512,512]{0,1:T(8,128)}, f32[]{:T(128)}, f32[512,512]{1,0:T(8,128)}, s32[]{:T(128)}) %tuple.39), condition=%wide.region_6.0_spmd.clone.clone, body=%wide.region_4.0_spmd.clone.clone.sunk | while | flops 12889620480 | bytes 33554572 | solution.py:52
  162.3 3.5 %convert_subtract_fusion.7 = f32[512,512]{0,1:T(8,128)S(1)} fusion(f32[512,512]{1,0:T(8,128)} %get-tuple-element.137, f32[512,512]{0,1:T(8,128)} %get-tuple-element.130), kind=kOutput, calls=%fused_computation.4.clone.1 | convolution fusion | flops 1611399168 | bytes 3145728 | tf_op jit(solution)/shard_map/while/body/dot_general | solution.py:41
  165.8 3.4 %fusion.87 = f32[512,512]{0,1:T(8,128)S(1)} fusion(f32[512,512]{0,1:T(8,128)} %get-tuple-element.130, f32[512,512]{0,1:T(8,128)S(1)} %convert_subtract_fusion.7), kind=kOutput, calls=%fused_computation.12.clone.1 | convolution fusion | flops 1610874880 | bytes 3145728 | tf_op jit(solution)/shard_map/while/body/dot_general | solution.py:43
  171.1 1.9 convolution_add_fusion.7
  173.0 1.9 convert_subtract_fusion.9
  174.8 1.9 convolution_add_fusion.8
  176.7 3.5 %multiply_reduce_fusion.3 = (f32[]{:T(128)}, f32[512,512]{0,1:T(8,128)}) fusion(f32[512,512]{0,1:T(8,128)S(1)} %convolution_add_fusion.8, f32[512,512]{1,0:T(8,128)S(1)} %copy-done.2), kind=kOutput, calls=%fused_computation.14.clone.1 | convolution fusion | flops 1611923456 | bytes 3145732 | tf_op jit(solution)/shard_map/while/body/dot_general | solution.py:41
  180.9 4.7 %convolution_add_fusion.9 = f32[512,512]{0,1:T(8,128)} fusion(f32[512,512]{0,1:T(8,128)} %copy-done.3, f32[512,512]{0,1:T(8,128)} %get-tuple-element.122), kind=kOutput, calls=%fused_computation.5.clone.1 | convolution fusion | flops 1610874880 | bytes 3145728 | tf_op jit(solution)/shard_map/while/body/dot_general | solution.py:43
  185.6 3.5 %convert_subtract_fusion.7 = f32[512,512]{0,1:T(8,128)S(1)} fusion(f32[512,512]{1,0:T(8,128)} %get-tuple-element.137, f32[512,512]{0,1:T(8,128)} %get-tuple-element.130), kind=kOutput, calls=%fused_computation.4.clone.1 | convolution fusion | flops 1611399168 | bytes 3145728 | tf_op jit(solution)/shard_map/while/body/dot_general | solution.py:41
  189.1 3.4 %fusion.87 = f32[512,512]{0,1:T(8,128)S(1)} fusion(f32[512,512]{0,1:T(8,128)} %get-tuple-element.130, f32[512,512]{0,1:T(8,128)S(1)} %convert_subtract_fusion.7), kind=kOutput, calls=%fused_computation.12.clone.1 | convolution fusion | flops 1610874880 | bytes 3145728 | tf_op jit(solution)/shard_map/while/body/dot_general | solution.py:43
  194.4 1.9 convolution_add_fusion.7
  196.3 1.9 convert_subtract_fusion.9
  198.2 1.9 convolution_add_fusion.8
  200.1 3.5 %multiply_reduce_fusion.3 = (f32[]{:T(128)}, f32[512,512]{0,1:T(8,128)}) fusion(f32[512,512]{0,1:T(8,128)S(1)} %convolution_add_fusion.8, f32[512,512]{1,0:T(8,128)S(1)} %copy-done.2), kind=kOutput, calls=%fused_computation.14.clone.1 | convolution fusion | flops 1611923456 | bytes 3145732 | tf_op jit(solution)/shard_map/while/body/dot_general | solution.py:41
  204.2 4.7 %convolution_add_fusion.9 = f32[512,512]{0,1:T(8,128)} fusion(f32[512,512]{0,1:T(8,128)} %copy-done.3, f32[512,512]{0,1:T(8,128)} %get-tuple-element.122), kind=kOutput, calls=%fused_computation.5.clone.1 | convolution fusion | flops 1610874880 | bytes 3145728 | tf_op jit(solution)/shard_map/while/body/dot_general | solution.py:43
  208.9 3.5 %convert_subtract_fusion.7 = f32[512,512]{0,1:T(8,128)S(1)} fusion(f32[512,512]{1,0:T(8,128)} %get-tuple-element.137, f32[512,512]{0,1:T(8,128)} %get-tuple-element.130), kind=kOutput, calls=%fused_computation.4.clone.1 | convolution fusion | flops 1611399168 | bytes 3145728 | tf_op jit(solution)/shard_map/while/body/dot_general | solution.py:41
  212.4 3.4 %fusion.87 = f32[512,512]{0,1:T(8,128)S(1)} fusion(f32[512,512]{0,1:T(8,128)} %get-tuple-element.130, f32[512,512]{0,1:T(8,128)S(1)} %convert_subtract_fusion.7), kind=kOutput, calls=%fused_computation.12.clone.1 | convolution fusion | flops 1610874880 | bytes 3145728 | tf_op jit(solution)/shard_map/while/body/dot_general | solution.py:43
  217.7 1.9 convolution_add_fusion.7
  221.5 1.9 convolution_add_fusion.8
  223.4 3.5 %multiply_reduce_fusion.3 = (f32[]{:T(128)}, f32[512,512]{0,1:T(8,128)}) fusion(f32[512,512]{0,1:T(8,128)S(1)} %convolution_add_fusion.8, f32[512,512]{1,0:T(8,128)S(1)} %copy-done.2), kind=kOutput, calls=%fused_computation.14.clone.1 | convolution fusion | flops 1611923456 | bytes 3145732 | tf_op jit(solution)/shard_map/while/body/dot_general | solution.py:41
  227.5 4.7 %convolution_add_fusion.9 = f32[512,512]{0,1:T(8,128)} fusion(f32[512,512]{0,1:T(8,128)} %copy-done.3, f32[512,512]{0,1:T(8,128)} %get-tuple-element.122), kind=kOutput, calls=%fused_computation.5.clone.1 | convolution fusion | flops 1610874880 | bytes 3145728 | tf_op jit(solution)/shard_map/while/body/dot_general | solution.py:43
  232.3 3.1 %fusion.23 = f32[512,256]{1,0:T(8,128)S(1)} fusion(f32[512,512]{0,1:T(8,128)} %get-tuple-element.44, f32[512,256]{1,0:T(8,128)S(1)} %fusion.3), kind=kOutput, calls=%fused_computation.49 | convolution fusion | flops 805306368 | bytes 2097152 | tf_op jit(solution)/shard_map/dot_general | solution.py:55
  235.4 2.2 convolution_subtract_fusion
  (52 shorter events, 19.6 us)
Async XLA Ops:
  6.5 3.2 %copy-start = (bf16[1,96,14336]{2,1,0:T(8,128)(2,1)S(1)}, bf16[1,96,14336]{2,1,0:T(8,128)(2,1)}, u32[]{:S(2)}) copy-start(bf16[1,96,14336]{2,1,0:T(8,128)(2,1)} %param.14) | copy-start | bytes 8257540
  6.5 117.8 %all-gather.3.cloned.1.call-start = ((), (), s32[]{:S(2)}) async-start(), calls=%async_computation | async-start | bytes 13369344 | tf_op jit(solution)/shard_map/all_gather | solution.py:77
  12.5 5.2 %copy-start.7 = (bf16[4096,64]{0,1:T(8,128)(2,1)S(1)}, bf16[4096,64]{0,1:T(8,128)(2,1)}, u32[]{:S(2)}) copy-start(bf16[4096,64]{0,1:T(8,128)(2,1)} %param.16) | copy-start | bytes 1572868
  128.3 15.9 %copy-start.5 = (f32[256,4096]{1,0:T(8,128)}, f32[256,4096]{1,0:T(8,128)S(1)}, u32[]{:S(2)}) copy-start(f32[256,4096]{1,0:T(8,128)S(1)} %get-tuple-element.90) | copy-start | bytes 12582916
  128.4 15.9 %copy-start.6 = (f32[256,4096]{1,0:T(8,128)}, f32[256,4096]{1,0:T(8,128)S(1)}, u32[]{:S(2)}) copy-start(f32[256,4096]{1,0:T(8,128)S(1)} %get-tuple-element.91) | copy-start | bytes 12582916
  146.3 10.7 %copy-start.1 = (f32[512,512]{1,0:T(8,128)}, f32[512,512]{1,0:T(8,128)S(1)}, u32[]{:S(2)}) copy-start(f32[512,512]{1,0:T(8,128)S(1)} %select_add_fusion) | copy-start | bytes 3145732
  162.3 6.9 %copy-start.2 = (f32[512,512]{1,0:T(8,128)S(1)}, f32[512,512]{1,0:T(8,128)}, u32[]{:S(2)}) copy-start(f32[512,512]{1,0:T(8,128)} %get-tuple-element.137) | copy-start | bytes 3145732 | tf_op jit(solution)/shard_map/while
  176.7 3.5 %copy-start.3 = (f32[512,512]{0,1:T(8,128)}, f32[512,512]{0,1:T(8,128)S(1)}, u32[]{:S(2)}) copy-start(f32[512,512]{0,1:T(8,128)S(1)} %convolution_add_fusion.8) | copy-start | bytes 3145732 | tf_op jit(solution)/shard_map/while
  185.6 6.9 %copy-start.2 = (f32[512,512]{1,0:T(8,128)S(1)}, f32[512,512]{1,0:T(8,128)}, u32[]{:S(2)}) copy-start(f32[512,512]{1,0:T(8,128)} %get-tuple-element.137) | copy-start | bytes 3145732 | tf_op jit(solution)/shard_map/while
  200.0 3.5 %copy-start.3 = (f32[512,512]{0,1:T(8,128)}, f32[512,512]{0,1:T(8,128)S(1)}, u32[]{:S(2)}) copy-start(f32[512,512]{0,1:T(8,128)S(1)} %convolution_add_fusion.8) | copy-start | bytes 3145732 | tf_op jit(solution)/shard_map/while
  208.9 6.9 %copy-start.2 = (f32[512,512]{1,0:T(8,128)S(1)}, f32[512,512]{1,0:T(8,128)}, u32[]{:S(2)}) copy-start(f32[512,512]{1,0:T(8,128)} %get-tuple-element.137) | copy-start | bytes 3145732 | tf_op jit(solution)/shard_map/while
  223.4 3.5 %copy-start.3 = (f32[512,512]{0,1:T(8,128)}, f32[512,512]{0,1:T(8,128)S(1)}, u32[]{:S(2)}) copy-start(f32[512,512]{0,1:T(8,128)S(1)} %convolution_add_fusion.8) | copy-start | bytes 3145732 | tf_op jit(solution)/shard_map/while
  232.3 5.3 %copy-start.4 = (f32[512,512]{0,1:T(8,128)S(1)}, f32[512,512]{0,1:T(8,128)}, u32[]{:S(2)}) copy-start(f32[512,512]{0,1:T(8,128)} %get-tuple-element.44) | copy-start | bytes 3145732
Sparse Core Ops, SparseCore 0:
  42.2 82.0 all-gather.2
where the time goes:
time: 247 us
  matrix products  113 us (46%)
  waiting for transfers between devices  82.2 us (33%)
  blocking collectives  20.5 us (8%)
  between operations  14.3 us (6%)
  local copies, waits for them, and re-layouts  8.45 us (3%)
  other arithmetic  6.29 us (3%)
    all_gather x1, waiting for transfers between devices, body(): everyone = lax.all_gather(within, AXES[0], axis=0, tiled=True)  82.2 us
    dot_general x12, matrix products, one_step(): return (inverse + jnp.dot(inverse, remainder, precision=HIGHEST), residual)  35.7 us
    dot_general x12, matrix products, one_step(): remainder = eye - jnp.dot(system, inverse, precision=HIGHEST)  32.1 us
    all_gather x1, blocking collectives, body(): within = lax.all_gather(both.reshape(1, -1), AXES[1], axis=0, tiled=True)  20.5 us
    dot_general x1, matrix products, body(): gram_matrix = jnp.dot(all_train, all_train.T, precision=HIGHEST)  15.9 us
    dot_general x1, matrix products, body(): products = jnp.dot(all_train, pieces[block_rows].T, precision=HIGHEST)  10.6 us
    dot_general x2, matrix products, sketch_terms(): jnp.dot(outgrad.reshape(proof_count * token_count, -1), proj_out, preferr...  7.41 us
  transfers between devices with their start and end apart: 1, of which 1 were waited for; matrix products, arithmetic and copies ran while one was open for 0% of the time, Pallas kernels for 0%

commit v1 on v0

--- a/solution.py
+++ b/solution.py
@@ -6,6 +6,11 @@
 damping_share = 0.1
 AXES = ("train", "query")
 HIGHEST = lax.Precision.HIGHEST
+
+
+def gather_over(x, name, dim):
+    stack = jnp.stack([x] * lax.axis_size(name))
+    return jnp.concatenate(lax.all_to_all(stack, name, 0, 0), axis=dim)
 
 
 def sketch_terms(hidden, outgrad, mask, proj_in, proj_out):
@@ -74,7 +79,7 @@
     width = train_sketch.shape[1]
     both = jnp.concatenate([train_sketch, query_sketch], axis=0)
     within = lax.all_gather(both.reshape(1, -1), AXES[1], axis=0, tiled=True)
-    everyone = lax.all_gather(within, AXES[0], axis=0, tiled=True)
+    everyone = gather_over(within, AXES[0], 0)
     devices = everyone.shape[0]
     pieces = [everyone[:, r * width : (r + 1) * width] for r in range(block_rows + 1)]
     all_train = jnp.concatenate(pieces[:block_rows], axis=0)

time: 247 us -> 453 us (1.83); the launches traced: 247 us -> 445 us
  waiting for transfers between devices: 82.2 us -> 273 us
  starting transfers between devices: 0.01 us -> 14.3 us
  between operations: 14.3 us -> 1.01 us
  loops' own time: 2.19 us -> 12.6 us
  matrix products: 113 us -> 104 us
  local copies, waits for them, and re-layouts: 8.45 us -> 14.3 us
    all_to_all x0 -> x1, waiting for transfers between devices: none -> 273 us  [gather_over(): return jnp.concatenate(lax.all_to_all(stack, name, 0, 0), axis=dim)]
    all_gather x1 -> x0, waiting for transfers between devices: 82.2 us -> none  [body(): everyone = lax.all_gather(within, AXES[0], axis=0, tiled=True)]
    all_to_all x0 -> x1, starting transfers between devices: none -> 14.3 us  [gather_over(): return jnp.concatenate(lax.all_to_all(stack, name, 0, 0), axis=dim)]
    another operation x1, loops' own time: 2.19 us -> 12.6 us  [spd_solve(): lax.while_loop(going, advance, (jnp.int32(0), start, jnp.array(jnp.inf, s...]
    another operation x0 -> x1, local copies, waits for them, and re-layouts: none -> 5.89 us  [gather_over(): stack = jnp.stack([x] * lax.axis_size(name))]
    dot_general x12, matrix products: 35.7 us -> 30.5 us  [one_step(): return (inverse + jnp.dot(inverse, remainder, precision=HIGHEST), residual)]
where the time goes in v1:
time: 453 us; the launch traced here: 445 us
  waiting for transfers between devices  273 us (60%)
  matrix products  104 us (23%)
  blocking collectives  20.3 us (4%)
  local copies, waits for them, and re-layouts  14.3 us (3%)
  starting transfers between devices  14.3 us (3%)
  loops' own time  12.6 us (3%)
  other arithmetic  5.72 us (1%)
    all_to_all x1, waiting for transfers between devices, gather_over(): return jnp.concatenate(lax.all_to_all(stack, name, 0, 0), axis=dim)  273 us
    dot_general x12, matrix products, one_step(): return (inverse + jnp.dot(inverse, remainder, precision=HIGHEST), residual)  30.5 us
    dot_general x12, matrix products, one_step(): remainder = eye - jnp.dot(system, inverse, precision=HIGHEST)  29.4 us
    all_gather x1, blocking collectives, body(): within = lax.all_gather(both.reshape(1, -1), AXES[1], axis=0, tiled=True)  20.3 us
    dot_general x1, matrix products, body(): gram_matrix = jnp.dot(all_train, all_train.T, precision=HIGHEST)  16.3 us
    all_to_all x1, starting transfers between devices, gather_over(): return jnp.concatenate(lax.all_to_all(stack, name, 0, 0), axis=dim)  14.3 us
    another operation x1, loops' own time, spd_solve(): lax.while_loop(going, advance, (jnp.int32(0), start, jnp.array(jnp.inf, s...  12.6 us
  transfers between devices with their start and end apart: 1, of which 1 were waited for; matrix products, arithmetic and copies ran while one was open for 0% of the time, Pallas kernels for 0%

profile of v1, /device:TPU:1, one launch (start us, length us, event | category | flops | bytes accessed | tf_op | source)
XLA Modules:
  0.0 445.1 jit_solution(8024454383910993749)
XLA Ops:
  0.9 5.0 %convolution_multiply_fusion = f32[192,64]{0,1:T(8,128)S(1)} fusion(bf16[192,14336]{1,0:T(8,128)(2,1)} %bitcast.104, bf16[14336,64]{0,1:T(8,128)(2,1)} %param.17, f32[192]{0:T(256)S(1)} %convert_element_type.33), kind=kOutput, calls=%fused_computation.24 | convolution fusion | flops 352333824 | bytes 7389952 | tf_op jit(solution)/shard_map/dot_general | solution.py:23
  6.1 2.1 fusion.15
  10.1 2.4 fusion.9
  12.9 20.3 %all-gather = f32[16,1,12288]{2,1,0:T(1,128)S(1)} all-gather(f32[1,1,12288]{2,1,0:T(1,128)S(1)} %reshape.74), channel_id=1, replica_groups=mesh['train'=16,'query'=16] {'query'}, dimensions={0}, use_global_device_ids=true | all-gather | bytes 835584 | tf_op jit(solution)/shard_map/all_gather | solution.py:81
  33.6 5.9 %stack.2 = f32[16,16,12288]{2,1,0:T(8,128)} broadcast(f32[16,12288]{1,0:T(8,128)S(1)} %bitcast.105), dimensions={1,2} | broadcast | bytes 13369344 | tf_op jit(solution)/shard_map/stack | solution.py:12
  39.5 14.3 %all-to-all-start = ((f32[16,16,12288]{2,1,0:T(8,128)}), f32[16,16,12288]{2,1,0:T(8,128)}, u32[]{:S(2)}, u32[]{:S(2)}) async-start(f32[16,16,12288]{2,1,0:T(8,128)} %stack.2), calls=%async_computation | async-start | bytes 25165824 | tf_op jit(solution)/shard_map/all_to_all | solution.py:13
  53.9 273.2 %all-to-all-done = f32[16,16,12288]{2,1,0:T(8,128)} async-done(((f32[16,16,12288]{2,1,0:T(8,128)}), f32[16,16,12288]{2,1,0:T(8,128)}, u32[]{:S(2)}, u32[]{:S(2)}) %all-to-all-start) | async-done | bytes 12582944 | tf_op jit(solution)/shard_map/all_to_all | solution.py:13
  327.0 4.0 fusion.21
  331.1 16.3 %select_reduce_fusion.1 = (f32[]{:T(128)}, f32[512,512]{1,0:T(8,128)}) fusion(f32[256,4096]{1,0:T(8,128)S(1)} %get-tuple-element.91, f32[256,4096]{1,0:T(8,128)S(1)} %get-tuple-element.90), kind=kOutput, calls=%fused_computation.29 | convolution fusion | flops 12887785472 | bytes 9437188 | tf_op jit(solution)/shard_map/dot_general | solution.py:86
  347.3 9.0 %fusion.3 = f32[512,256]{1,0:T(8,128)S(1)} fusion(f32[256,4096]{1,0:T(8,128)S(1)} %get-tuple-element.91, f32[256,4096]{1,0:T(8,128)S(1)} %get-tuple-element.90, f32[256,12288]{1,0:T(8,128)} %bitcast.5), kind=kOutput, calls=%fused_computation.16 | convolution fusion | flops 6444548096 | bytes 13107200 | tf_op jit(solution)/shard_map/dot_general | solution.py:87
  362.0 2.6 copy.18
  364.6 72.5 %while.14 = (s32[]{:T(128)}, f32[512,512]{0,1:T(8,128)}, f32[]{:T(128)}, f32[512,512]{1,0:T(8,128)}, s32[]{:T(128)}) while((s32[]{:T(128)}, f32[512,512]{0,1:T(8,128)}, f32[]{:T(128)}, f32[512,512]{1,0:T(8,128)}, s32[]{:T(128)}) %tuple.37), condition=%wide.region_6.0_spmd.clone.clone, body=%wide.region_4.0_spmd.clone.clone.sunk | while | flops 12889620480 | bytes 29360240 | solution.py:57
  374.8 3.5 convert_subtract_fusion.7
  378.3 3.5 fusion.87
  383.7 1.9 convolution_add_fusion.7
  387.4 1.9 convolution_add_fusion.8
  389.3 2.6 multiply_reduce_fusion.3
  391.9 2.9 convolution_add_fusion.9
  395.5 3.5 convert_subtract_fusion.7
  399.0 3.5 fusion.87
  404.4 1.9 convolution_add_fusion.7
  408.2 1.9 convolution_add_fusion.8
  410.0 2.6 multiply_reduce_fusion.3
  412.6 2.9 convolution_add_fusion.9
  416.2 3.5 convert_subtract_fusion.7
  419.7 3.5 fusion.87
  425.1 1.9 convolution_add_fusion.7
  428.9 1.9 convolution_add_fusion.8
  430.8 2.6 multiply_reduce_fusion.3
  433.4 2.9 convolution_add_fusion.9
  437.1 3.1 fusion.23
  440.3 2.2 convolution_subtract_fusion
  (44 shorter events, 22.4 us)
Async XLA Ops:
  0.0 10.0 %copy-start = (bf16[1,96,14336]{2,1,0:T(8,128)(2,1)S(1)}, bf16[1,96,14336]{2,1,0:T(8,128)(2,1)}, u32[]{:S(2)}) copy-start(bf16[1,96,14336]{2,1,0:T(8,128)(2,1)} %param.14) | copy-start | bytes 8257540
  0.9 5.2 %copy-start.4 = (bf16[4096,64]{0,1:T(8,128)(2,1)S(1)}, bf16[4096,64]{0,1:T(8,128)(2,1)}, u32[]{:S(2)}) copy-start(bf16[4096,64]{0,1:T(8,128)(2,1)} %param.16) | copy-start | bytes 1572868
  0.9 7.6 %copy-start.5 = (s32[1,96]{1,0:T(1,128)S(1)}, s32[1,96]{1,0:T(1,128)}, u32[]{:S(2)}) copy-start(s32[1,96]{1,0:T(1,128)} %param.15) | copy-start | bytes 1156
  39.5 287.5 %all-to-all-start = ((f32[16,16,12288]{2,1,0:T(8,128)}), f32[16,16,12288]{2,1,0:T(8,128)}, u32[]{:S(2)}, u32[]{:S(2)}) async-start(f32[16,16,12288]{2,1,0:T(8,128)} %stack.2), calls=%async_computation | async-start | bytes 25165824 | tf_op jit(solution)/shard_map/all_to_all | solution.py:13
  358.2 1.0 copy-start.1
  374.8 7.0 %copy-start.2 = (f32[512,512]{1,0:T(8,128)S(1)}, f32[512,512]{1,0:T(8,128)}, u32[]{:S(2)}) copy-start(f32[512,512]{1,0:T(8,128)} %get-tuple-element.137) | copy-start | bytes 3145732 | tf_op jit(solution)/shard_map/while
  395.5 7.0 %copy-start.2 = (f32[512,512]{1,0:T(8,128)S(1)}, f32[512,512]{1,0:T(8,128)}, u32[]{:S(2)}) copy-start(f32[512,512]{1,0:T(8,128)} %get-tuple-element.137) | copy-start | bytes 3145732 | tf_op jit(solution)/shard_map/while
  416.2 7.0 %copy-start.2 = (f32[512,512]{1,0:T(8,128)S(1)}, f32[512,512]{1,0:T(8,128)}, u32[]{:S(2)}) copy-start(f32[512,512]{1,0:T(8,128)} %get-tuple-element.137) | copy-start | bytes 3145732 | tf_op jit(solution)/shard_map/while
  437.1 5.4 %copy-start.3 = (f32[512,512]{0,1:T(8,128)S(1)}, f32[512,512]{0,1:T(8,128)}, u32[]{:S(2)}) copy-start(f32[512,512]{0,1:T(8,128)} %get-tuple-element.44) | copy-start | bytes 3145732
